TPU v7x, 128 devices: a whole 4x4x4 slice. The times are simulated.
128 devices in a mesh: row: 16 (over z_hi, x, core), col: 8 (over y, z_lo).
Axes of the slice: x: 4, y: 4, z: 4 (z_hi: 2, z_lo: 2; z = z_hi * 2 + z_lo), core: 2. Of those that a mesh axis runs over, the one named last changes fastest.
Arguments:
- before_scan: float32 [4, 4096, 8192], P(None, 'row', 'col'), may hold values from -40 to 40
- after_scan: float32 [4, 4096, 8192], P(None, 'row', 'col'), may hold values from -40 to 40
- drift_offsets: int32 [2, 4, 16, 8], P(None, None, 'row', 'col'), may hold values from -128 to 128, as said below
- drift_fractions: int32 [2, 4, 16, 8], P(None, None, 'row', 'col'), may hold values from 0 to 255
Outputs:
- band_field: float32 [4, 4096, 8192], P(None, 'row', 'col')
- slope_field: float32 [4, 4096, 8192], P(None, 'row', 'col')
- surface_params: float32 [2, 4], replicated
Inputs may be any that keep to these rules, and one draw needn't show every extreme that they name: `drift_offsets`: for every scan and tile, the cells a tile reads (its own cells shifted by its offsets, widened by one row and column before and two after) lie inside the window. In every scan the first tile has offsets 128, 128 and the last tile minus 128, minus 128.
All inputs are finite; a program needn't handle non-finite values.
Results may differ from a plain program's by a relative error of at most 0.00014.
Values sent between devices are 32-bit elements; how exact they have to be, the bound alone decides.
No kernel may reach another device: no remote copies, remote signals or barrier semaphores. Data moves between devices by JAX's collectives and lax.ppermute only.
A program may use at most 128 MiB of HBM per device.

v0:
```python
import math
import jax
import jax.numpy as jnp
from jax import lax
from jax.sharding import PartitionSpec as P

LS = 5
SR = 4
LCUT = 1600
BLOCK = 16
DRIFT = 128
ALPHA = math.sqrt(math.log(2.0) / math.pi)
SPACING = 0.5
EPSILON = 1e-06
HIGHEST = lax.Precision.HIGHEST


def with_halo(value, sides, width):
    for axis, dim in sides:
        count, length = (lax.axis_size(axis), value.shape[dim])
        up = [(i, (i + 1) % count) for i in range(count - 1)]
        down = [(j, i) for i, j in up]
        last = lax.slice_in_dim(value, length - width, length, axis=dim)
        leading = lax.slice_in_dim(value, 0, width, axis=dim)
        before = lax.ppermute(last, axis, up)
        after = lax.ppermute(leading, axis, down)
        value = jnp.concatenate([before, value, after], axis=dim)
    return value


def cubic_weights(fraction):
    position = fraction.astype(jnp.float32) / 256.0
    square = position * position
    cube_term = square * position
    return (
        0.5 * (2.0 * square - cube_term - position),
        0.5 * (3.0 * cube_term - 5.0 * square + 2.0),
        0.5 * (4.0 * square - 3.0 * cube_term + position),
        0.5 * (cube_term - square),
    )


def interpolate(window, row_taps, col_taps):
    height = window.shape[0] - 3
    length = window.shape[1] - 3
    across = (
        row_taps[0] * window[0:height]
        + row_taps[1] * window[1 : height + 1]
        + row_taps[2] * window[2 : height + 2]
        + row_taps[3] * window[3 : height + 3]
    )
    return (
        col_taps[0] * across[:, 0:length]
        + col_taps[1] * across[:, 1 : length + 1]
        + col_taps[2] * across[:, 2 : length + 2]
        + col_taps[3] * across[:, 3 : length + 3]
    )


def resample(after_scan, drift_offsets, drift_fractions):
    height, length = (after_scan.shape[1], after_scan.shape[2])
    margin = DRIFT + 2
    widened = with_halo(after_scan, (("row", 1), ("col", 2)), margin)
    row_taps = jnp.stack(cubic_weights(drift_fractions[0, :, 0, 0]), axis=-1)
    col_taps = jnp.stack(cubic_weights(drift_fractions[1, :, 0, 0]), axis=-1)

    def one_scan(window, row_shift, col_shift, row_weights, col_weights):
        source = lax.dynamic_slice(
            window, (margin - 1 + row_shift, margin - 1 + col_shift), (height + 3, length + 3)
        )
        return interpolate(source, row_weights, col_weights)

    return jax.vmap(one_scan)(
        widened, drift_offsets[0, :, 0, 0], drift_offsets[1, :, 0, 0], row_taps, col_taps
    )


def short_taps():
    return [math.exp(-math.pi * (offset / (ALPHA * LS)) ** 2) for offset in range(-SR, SR + 1)]


def short_filter(widened, height, length):
    kernel_taps = short_taps()
    column_index = (
        lax.axis_index("col") * length - SR + jnp.arange(length + 2 * SR, dtype=jnp.int32)
    )
    column_inside = ((column_index >= 0) & (column_index < length * lax.axis_size("col"))).astype(
        jnp.float32
    )
    summed = kernel_taps[0] * widened[:, :, 0:length]
    weight = kernel_taps[0] * column_inside[0:length]
    for offset in range(1, 2 * SR + 1):
        summed = summed + kernel_taps[offset] * widened[:, :, offset : offset + length]
        weight = weight + kernel_taps[offset] * column_inside[offset : offset + length]
    across = summed / weight
    row_index = lax.axis_index("row") * height - SR + jnp.arange(height + 2 * SR, dtype=jnp.int32)
    row_inside = ((row_index >= 0) & (row_index < height * lax.axis_size("row"))).astype(
        jnp.float32
    )
    summed = kernel_taps[0] * across[:, 0:height, :]
    weight = kernel_taps[0] * row_inside[0:height]
    for offset in range(1, 2 * SR + 1):
        summed = summed + kernel_taps[offset] * across[:, offset : offset + height, :]
        weight = weight + kernel_taps[offset] * row_inside[offset : offset + height]
    return summed / weight[:, None]


def coarse_means(surface):
    scans, height, length = surface.shape
    return surface.reshape(scans, height // BLOCK, BLOCK, length // BLOCK, BLOCK).mean(axis=(2, 4))


def gauss_block(source, target):
    distance = ((source[:, None] - target[None, :]) * BLOCK).astype(jnp.float32) / (ALPHA * LCUT)
    return jnp.exp(-math.pi * distance * distance)


def long_cols(coarse):
    width = coarse.shape[2]
    target = lax.axis_index("col") * width + jnp.arange(width, dtype=jnp.int32)
    portion = lax.all_gather(coarse, "col", axis=2, tiled=True)
    source = jnp.arange(portion.shape[2], dtype=jnp.int32)
    matrix = gauss_block(source, target)
    summed = jnp.einsum("frk,kc->frc", portion, matrix, precision=HIGHEST)
    weight = jnp.sum(matrix, axis=0)
    return summed / weight


def long_rows(surface):
    rows_here = surface.shape[1]
    target = lax.axis_index("row") * rows_here + jnp.arange(rows_here, dtype=jnp.int32)
    portion = lax.all_gather(surface, "row", axis=1, tiled=True)
    source = jnp.arange(portion.shape[1], dtype=jnp.int32)
    matrix = gauss_block(target, source)
    summed = jnp.einsum("rk,fkc->frc", matrix, portion, precision=HIGHEST)
    weight = jnp.sum(matrix, axis=1)
    return summed / weight[:, None]


def upsample_matrix(fine_index, coarse_index, coarse_count):
    numerator = 2 * fine_index + 1 - BLOCK
    lower_index = numerator // (2 * BLOCK)
    fraction = (numerator - lower_index * (2 * BLOCK)).astype(jnp.float32) / (2.0 * BLOCK)
    outside = (lower_index < 0) | (lower_index >= coarse_count - 1)
    fraction = jnp.where(outside, jnp.zeros_like(fraction), fraction)
    lower_index = jnp.clip(lower_index, 0, coarse_count - 1)
    first_part = (coarse_index[None, :] == lower_index[:, None]).astype(jnp.float32) * (
        1.0 - fraction
    )[:, None]
    second_part = (coarse_index[None, :] == (lower_index + 1)[:, None]).astype(
        jnp.float32
    ) * fraction[:, None]
    return first_part + second_part


def upsample(wavy_coarse, height, length):
    coarse_rows, coarse_cols = (wavy_coarse.shape[1], wavy_coarse.shape[2])
    widened_coarse = with_halo(wavy_coarse, (("row", 1), ("col", 2)), 1)
    row_fine = lax.axis_index("row") * height + jnp.arange(height, dtype=jnp.int32)
    row_blocks = (
        lax.axis_index("row") * coarse_rows - 1 + jnp.arange(coarse_rows + 2, dtype=jnp.int32)
    )
    col_fine = lax.axis_index("col") * length + jnp.arange(length, dtype=jnp.int32)
    col_blocks = (
        lax.axis_index("col") * coarse_cols - 1 + jnp.arange(coarse_cols + 2, dtype=jnp.int32)
    )
    row_up = upsample_matrix(row_fine, row_blocks, coarse_rows * lax.axis_size("row"))
    col_up = upsample_matrix(col_fine, col_blocks, coarse_cols * lax.axis_size("col"))
    row_mixed = jnp.einsum("pa,sab->spb", row_up, widened_coarse, precision=HIGHEST)
    return jnp.einsum("spb,qb->spq", row_mixed, col_up, precision=HIGHEST)


def slopes(surface):
    height, length = (surface.shape[1], surface.shape[2])
    bordered = with_halo(surface, (("row", 1), ("col", 2)), 1)
    column_index = lax.axis_index("col") * length + jnp.arange(length, dtype=jnp.int32)
    row_index = lax.axis_index("row") * height + jnp.arange(height, dtype=jnp.int32)
    column_mask = (
        (column_index >= 1) & (column_index <= length * lax.axis_size("col") - 2)
    ).astype(jnp.float32)
    row_mask = ((row_index >= 1) & (row_index <= height * lax.axis_size("row") - 2)).astype(
        jnp.float32
    )
    along_cols = (bordered[:, 1:-1, 2:] - bordered[:, 1:-1, :-2]) / (2.0 * SPACING) * column_mask
    along_rows = (
        (bordered[:, 2:, 1:-1] - bordered[:, :-2, 1:-1]) / (2.0 * SPACING) * row_mask[:, None]
    )
    return along_cols * along_cols + along_rows * along_rows


def body(before_scan, after_scan, drift_offsets, drift_fractions):
    height, length = (before_scan.shape[1], before_scan.shape[2])
    shifted = resample(after_scan, drift_offsets, drift_fractions)
    difference = before_scan - shifted
    widened = with_halo(difference, (("row", 1), ("col", 2)), SR)
    smooth = short_filter(widened, height, length)
    coarse = coarse_means(smooth)
    wavy_coarse = long_rows(long_cols(coarse))
    waviness = upsample(wavy_coarse, height, length)
    band_field = smooth - waviness
    slope_field = slopes(band_field)
    height_sq = jnp.sum(band_field * band_field, axis=(1, 2))
    slope_sum = jnp.sum(slope_field, axis=(1, 2))
    height_all, slope_all = lax.psum((height_sq, slope_sum), ("row", "col"))
    total_cells = height * lax.axis_size("row") * length * lax.axis_size("col")
    surface_params = jnp.sqrt(jnp.stack([height_all, slope_all]) / total_cells + EPSILON)
    return (band_field, slope_field, surface_params)


def solution(mesh):
    in_specs = (
        P(None, "row", "col"),
        P(None, "row", "col"),
        P(None, None, "row", "col"),
        P(None, None, "row", "col"),
    )
    out_specs = (P(None, "row", "col"), P(None, "row", "col"), P())
    return jax.shard_map(body, mesh=mesh, in_specs=in_specs, out_specs=out_specs, check_vma=False)
```

profile of v0, /device:TPU:1, one launch (start us, length us, event | category | flops | bytes accessed | tf_op | source)
XLA Modules:
  0.0 455.7 jit_solution(10664465496469987918)
XLA Ops:
  5.3 4.5 collective-permute-start
  14.5 5.2 %copy.28 = f32[4,256,1024]{1,0,2:T(4,128)} copy(f32[4,256,1024]{2,1,0:T(8,128)} %param.5) | data formatting | bytes 8388608 | tf_op args[1]
  19.9 13.1 %collective-permute-done = f32[4,130,1024]{2,0,1:T(4,128)} collective-permute-done((f32[4,130,1024]{2,0,1:T(4,128)S(1)}, f32[4,130,1024]{2,0,1:T(4,128)}, u32[]{:S(2)}, u32[]{:S(2)}) %collective-permute-start) | collective-permute-done | bytes 2129952 | tf_op jit(solution)/shard_map/ppermute | solution.py:25
  33.1 6.2 %copy.27 = f32[4,130,1024]{1,0,2:T(4,128)} copy(f32[4,130,1024]{2,0,1:T(4,128)} %collective-permute-done) | data formatting | bytes 4259840 | tf_op jit(solution)/shard_map/ppermute | solution.py:25
  40.6 6.2 %copy.29 = f32[4,130,1024]{1,0,2:T(4,128)} copy(f32[4,130,1024]{2,0,1:T(4,128)} %collective-permute-done.1) | data formatting | bytes 4259840 | tf_op jit(solution)/shard_map/ppermute | solution.py:26
  46.8 3.5 pad_maximum_fusion.13
  50.3 3.8 collective-permute-start.2
  56.2 40.7 %collective-permute-done.2 = f32[4,516,130]{1,0,2:T(4,128)S(1)} collective-permute-done((f32[4,516,130]{1,0,2:T(4,128)S(1)}, f32[4,516,130]{1,0,2:T(4,128)S(1)}, u32[]{:S(2)}, u32[]{:S(2)}) %collective-permute-start.2) | collective-permute-done | bytes 1073312 | tf_op jit(solution)/shard_map/ppermute | solution.py:25
  97.0 29.5 %pad_maximum_fusion = f32[4,516,1284]{1,0,2:T(4,128)} fusion(f32[4,516,130]{1,0,2:T(4,128)S(1)} %collective-permute-done.3, f32[4,130,1024]{1,0,2:T(4,128)} %copy.29, f32[4,256,1024]{1,0,2:T(4,128)S(1)} %copy-done.2, f32[4,130,1024]{1,0,2:T(4,128)} %copy.27, f32[4,516,130]{1,0,2:T(4,128)S(1)} %collective-permute-done.2), kind=kLoop, calls=%fused_computation.2 | loop fusion | flops 10600704 | bytes 21201408 | tf_op jit(solution)/shard_map/concatenate | solution.py:27
  126.4 15.3 %copy.30 = f32[4,516,1284]{2,1,0:T(8,128)} copy(f32[4,516,1284]{1,0,2:T(4,128)} %pad_maximum_fusion) | data formatting | bytes 21201408
  141.7 21.6 %while.1 = (s32[]{:T(128)}, f32[4,516,1284]{2,1,0:T(8,128)}, s32[4,3]{1,0:T(4,128)S(1)}, f32[4,259,1027]{2,1,0:T(8,128)}, s32[]{:T(128)}) while((s32[]{:T(128)}, f32[4,516,1284]{2,1,0:T(8,128)}, s32[4,3]{1,0:T(4,128)S(1)}, f32[4,259,1027]{2,1,0:T(8,128)}, s32[]{:T(128)}) %tuple.51), condition=%wide.while_cond, body=%wide.while_body.sunk | while | flops 2 | bytes 2435185 | solution.py:68
  142.3 4.8 %dynamic-slice_dynamic-update-slice_fusion.2 = f32[4,259,1027]{2,1,0:T(8,128)} fusion(f32[4,259,1027]{2,1,0:T(8,128)} %get-tuple-element.118, s32[]{:T(128)} %get-tuple-element.115, f32[4,516,1284]{2,1,0:T(8,128)} %get-tuple-element.121, s32[]{:T(128)} %bitcast.84, s32[]{:T(128)} %bitcast.85, s32[]{:T(128)} %bitcast.86), kind=kLoop, calls=%fused_computation.clone.1 | loop fusion | bytes 2435072 | tf_op jit(solution)/shard_map/vmap()/gather
  147.8 4.7 %dynamic-slice_dynamic-update-slice_fusion.2 = f32[4,259,1027]{2,1,0:T(8,128)} fusion(f32[4,259,1027]{2,1,0:T(8,128)} %get-tuple-element.118, s32[]{:T(128)} %get-tuple-element.115, f32[4,516,1284]{2,1,0:T(8,128)} %get-tuple-element.121, s32[]{:T(128)} %bitcast.84, s32[]{:T(128)} %bitcast.85, s32[]{:T(128)} %bitcast.86), kind=kLoop, calls=%fused_computation.clone.1 | loop fusion | bytes 2435072 | tf_op jit(solution)/shard_map/vmap()/gather
  153.1 4.7 %dynamic-slice_dynamic-update-slice_fusion.2 = f32[4,259,1027]{2,1,0:T(8,128)} fusion(f32[4,259,1027]{2,1,0:T(8,128)} %get-tuple-element.118, s32[]{:T(128)} %get-tuple-element.115, f32[4,516,1284]{2,1,0:T(8,128)} %get-tuple-element.121, s32[]{:T(128)} %bitcast.84, s32[]{:T(128)} %bitcast.85, s32[]{:T(128)} %bitcast.86), kind=kLoop, calls=%fused_computation.clone.1 | loop fusion | bytes 2435072 | tf_op jit(solution)/shard_map/vmap()/gather
  158.5 4.7 %dynamic-slice_dynamic-update-slice_fusion.2 = f32[4,259,1027]{2,1,0:T(8,128)} fusion(f32[4,259,1027]{2,1,0:T(8,128)} %get-tuple-element.118, s32[]{:T(128)} %get-tuple-element.115, f32[4,516,1284]{2,1,0:T(8,128)} %get-tuple-element.121, s32[]{:T(128)} %bitcast.84, s32[]{:T(128)} %bitcast.85, s32[]{:T(128)} %bitcast.86), kind=kLoop, calls=%fused_computation.clone.1 | loop fusion | bytes 2435072 | tf_op jit(solution)/shard_map/vmap()/gather
  163.2 9.2 %multiply_add_fusion = f32[4,256,1027]{2,1,0:T(8,128)S(1)} fusion(f32[4,259,1027]{2,1,0:T(8,128)} %get-tuple-element.10, f32[4]{0:T(128)S(1)} %get-tuple-element.67, f32[4]{0:T(128)S(1)} %get-tuple-element.62, f32[4]{0:T(128)S(1)} %get-tuple-element.64, f32[4]{0:T(128)S(1)} %get-tuple-element.63), kind=kLoop, calls=%fused_computation.5 | loop fusion | flops 7361536 | bytes 21033024 | tf_op jit(solution)/shard_map/vmap()/add | solution.py:47
  172.5 3.4 fusion.25
  176.0 17.8 %collective-permute-start.4 = (f32[4,4,1024]{2,1,0:T(4,128)S(1)}, f32[4,4,1024]{2,1,0:T(4,128)S(1)}, u32[]{:S(2)}, u32[]{:S(2)}) collective-permute-start(f32[4,4,1024]{2,1,0:T(4,128)S(1)} %get-tuple-element.53), channel_id=1, source_target_pairs={{0,8},{8,16},{16,24},{24,32},{32,40},{40,48},{48,56},{56,64},{64,7... | collective-permute-start | bytes 196616 | tf_op jit(solution)/shard_map/ppermute | solution.py:25
  195.8 3.6 collective-permute-done.5
  200.4 4.1 collective-permute-start.6
  209.9 7.4 %maximum_maximum_fusion = (f32[4,264,1028]{2,1,0:T(8,128)S(1)}, f32[4,264,1028]{2,1,0:T(8,128)}) fusion(f32[4,4,1024]{2,1,0:T(4,128)S(1)} %collective-permute-done.5, f32[4,256,1024]{2,1,0:T(8,128)} %copy-done, f32[4,4,1024]{2,1,0:T(4,128)S(1)} %collective-permute-done.4, f32[4,264,4]{2,1,0:T(8,128)S(1)} %copy.33, f32[4,264,4]{2,1,0:T(8,128)S(1)} %copy.35), kind=kLoop, calls=%fused_computation.3 | loop fusion | flops 6513408 | bytes 13043712 | tf_op jit(solution)/shard_map/concatenate | solution.py:27
  217.3 15.3 %fusion.1 = f32[4,264,1024]{2,1,0:T(8,128)S(1)} fusion(f32[4,264,1028]{2,1,0:T(8,128)} %get-tuple-element.45, f32[4,264,1028]{2,1,0:T(8,128)S(1)} %get-tuple-element.44, f32[1024]{0:T(1024)S(1)} %fusion.80, f32[4,4,1024]{2,1,0:T(4,128)S(1)} %collective-permute-done.5, f32[4,256,1024]{2,1,0:T(8,128)} %copy-done, f32[4,4,1024]{2,1,0:T(4,128)S(1)} %collective-permute-done.4), kind=kLoop, calls=%fused_computation.8 | loop fusion | flops 20545536 | bytes 43257856 | tf_op jit(solution)/shard_map/div | solution.py:95
  232.7 5.7 %fusion.17 = f32[4,256,1024]{2,1,0:T(8,128)} fusion(f32[4,264,1024]{2,1,0:T(8,128)S(1)} %fusion.1, f32[256]{0:T(256)S(1)} %multiply_add_fusion.3), kind=kLoop, calls=%fused_computation.41 | loop fusion | flops 17825792 | bytes 41944064 | tf_op jit(solution)/shard_map/div | solution.py:105
  238.3 19.0 %reshape.249 = f32[4,16,16,64,16]{4,3,2,1,0:T(8,128)} reshape(f32[4,256,1024]{2,1,0:T(8,128)} %fusion.17) | data formatting | bytes 8388608 | tf_op jit(solution)/shard_map/reshape | solution.py:110
  257.3 12.2 %reduce_sum.45 = f32[4,16,64]{2,1,0:T(8,128)S(1)} reduce(f32[4,16,16,64,16]{4,3,2,1,0:T(8,128)} %reshape.249, f32[]{:T(128)} %constant.64.clone.1), dimensions={2,4}, to_apply=%region_0.0 | reduce | flops 1044480 | bytes 4210692 | tf_op jit(solution)/shard_map/reduce_sum | solution.py:110
  269.6 27.9 %all_gather.6 = f32[4,16,512]{1,0,2:T(4,128)S(1)} all-gather(f32[4,16,64]{1,0,2:T(4,128)S(1)} %copy.36), channel_id=1, replica_groups=mesh['row'=16,'col'=8] {'col'}, dimensions={2}, use_global_device_ids=true | all-gather | bytes 147456 | tf_op jit(solution)/shard_map/all_gather | solution.py:121
  299.3 27.6 %all_gather.7 = f32[4,256,64]{2,1,0:T(8,128)S(1)} all-gather(f32[4,16,64]{2,1,0:T(8,128)S(1)} %convolution_divide_fusion), channel_id=1, replica_groups=mesh['row'=16,'col'=8] {'row'}, dimensions={1}, use_global_device_ids=true | all-gather | bytes 278528 | tf_op jit(solution)/shard_map/all_gather | solution.py:132
  341.5 6.0 %convolution_subtract_fusion = f32[4,256,1024]{2,1,0:T(8,128)S(1)} fusion(f32[4,256,1024]{2,1,0:T(8,128)} %fusion.17, f32[4,256,66]{1,2,0:T(8,128)S(1)} %convolution_bitcast_fusion, f32[1024]{0:T(1024)S(1)} %get-tuple-element.71, s32[1024]{0:T(1024)S(1)} %get-tuple-element.74, f32[1024]{0:T(1024)S(1)} %get-tuple-element.72, ...), kind=kOutput, calls=%fused_computation.65 | convolution fusion | flops 831858688 | bytes 8675592 | tf_op jit(solution)/shard_map/spb,qb->spq/dot_general | solution.py:170
  347.5 3.4 collective-permute-start.12
  358.1 4.0 collective-permute-start.15
  363.0 13.9 %fusion.112 = (f32[4]{0:T(128)S(1)}, f32[4,256,1024]{2,1,0:T(8,128)}, f32[4]{0:T(128)S(1)}) fusion(f32[256]{0:T(256)S(1)} %and_convert_fusion, f32[4,256,1024]{2,1,0:T(8,128)} %copy-done.1, f32[4,1,1024]{2,1,0:T(1,128)S(1)} %collective-permute-done.12, f32[4,1,1024]{2,1,0:T(1,128)S(1)} %collective-permute-done.13, f32[1024]{0:T(1024)S(1)} %fusion.92, ...), kind=kLoop, calls=%fused_computation.219 | loop fusion | flops 18874360 | bytes 8434784 | tf_op jit(solution)/shard_map/reduce_sum | solution.py:203
  377.0 78.1 %all-reduce = (f32[1,4]{1,0:T(1,128)S(1)}, f32[1,4]{1,0:T(1,128)S(1)}) all-reduce(f32[1,4]{1,0:T(1,128)S(1)} %bitcast.87, f32[1,4]{1,0:T(1,128)S(1)} %bitcast.88), channel_id=1, replica_groups=mesh['row'=16,'col'=8] {'row','col'}, use_global_device_ids=true, to_apply=%region_6.7 | all-reduce | flops 8 | bytes 64 | tf_op jit(solution)/shard_map/psum | solution.py:204
  (90 shorter events, 48.9 us)
Async XLA Ops:
  5.3 27.8 %collective-permute-start = (f32[4,130,1024]{2,0,1:T(4,128)S(1)}, f32[4,130,1024]{2,0,1:T(4,128)}, u32[]{:S(2)}, u32[]{:S(2)}) collective-permute-start(f32[4,130,1024]{2,0,1:T(4,128)S(1)} %copy.42), channel_id=1, source_target_pairs={{0,8},{8,16},{16,24},{24,32},{32,40},{40,48},{48,56},{56,64},{64,7... | collective-permute-start | bytes 6389768 | tf_op jit(solution)/shard_map/ppermute | solution.py:25
  12.5 7.3 %copy-start.5 = (s32[2,4,1,1]{1,3,2,0:T(1,128)S(1)}, s32[2,4,1,1]{1,3,2,0:T(1,128)}, u32[]{:S(2)}) copy-start(s32[2,4,1,1]{1,3,2,0:T(1,128)} %param.6) | copy-start | bytes 100
  12.5 28.1 %collective-permute-start.1 = (f32[4,130,1024]{2,0,1:T(4,128)}, f32[4,130,1024]{2,0,1:T(4,128)}, u32[]{:S(2)}, u32[]{:S(2)}) collective-permute-start(f32[4,130,1024]{2,0,1:T(4,128)} %copy.43), channel_id=1, source_target_pairs={{8,0},{16,8},{24,16},{32,24},{40,32},{48,40},{56,48},{64,56},{72,6... | collective-permute-start | bytes 6389768 | tf_op jit(solution)/shard_map/ppermute | solution.py:26
  46.8 9.3 %copy-start.4 = (s32[2,4,1,1]{1,3,2,0:T(1,128)S(1)}, s32[2,4,1,1]{1,3,2,0:T(1,128)}, u32[]{:S(2)}) copy-start(s32[2,4,1,1]{1,3,2,0:T(1,128)} %param.7) | copy-start | bytes 100
  46.8 50.1 %copy-start.2 = (f32[4,256,1024]{1,0,2:T(4,128)S(1)}, f32[4,256,1024]{1,0,2:T(4,128)}, u32[]{:S(2)}) copy-start(f32[4,256,1024]{1,0,2:T(4,128)} %copy.28) | copy-start | bytes 12582916
  50.3 46.6 %collective-permute-start.2 = (f32[4,516,130]{1,0,2:T(4,128)S(1)}, f32[4,516,130]{1,0,2:T(4,128)S(1)}, u32[]{:S(2)}, u32[]{:S(2)}) collective-permute-start(f32[4,516,130]{1,0,2:T(4,128)S(1)} %get-tuple-element.42), channel_id=1, source_target_pairs={{0,1},{1,2},{2,3},{3,4},{4,5},{5,6},{6,7},{8,9},{9,10},{10,11},{11... | collective-permute-start | bytes 3219848 | tf_op jit(solution)/shard_map/ppermute | solution.py:25
  54.1 42.8 %collective-permute-start.3 = (f32[4,516,130]{1,0,2:T(4,128)S(1)}, f32[4,516,130]{1,0,2:T(4,128)S(1)}, u32[]{:S(2)}, u32[]{:S(2)}) collective-permute-start(f32[4,516,130]{1,0,2:T(4,128)S(1)} %get-tuple-element.43), channel_id=1, source_target_pairs={{1,0},{2,1},{3,2},{4,3},{5,4},{6,5},{7,6},{9,8},{10,9},{11,10},{12... | collective-permute-start | bytes 3219848 | tf_op jit(solution)/shard_map/ppermute | solution.py:26
  163.2 9.2 %copy-start.3 = (f32[4,256,1024]{2,1,0:T(8,128)S(1)}, f32[4,256,1024]{2,1,0:T(8,128)}, u32[]{:S(2)}) copy-start(f32[4,256,1024]{2,1,0:T(8,128)} %param.4) | copy-start | bytes 12582916
  175.9 24.1 %copy-start = (f32[4,256,1024]{2,1,0:T(8,128)}, f32[4,256,1024]{2,1,0:T(8,128)S(1)}, u32[]{:S(2)}) copy-start(f32[4,256,1024]{2,1,0:T(8,128)S(1)} %fusion.25) | copy-start | bytes 12582916
  176.0 19.8 %collective-permute-start.4 = (f32[4,4,1024]{2,1,0:T(4,128)S(1)}, f32[4,4,1024]{2,1,0:T(4,128)S(1)}, u32[]{:S(2)}, u32[]{:S(2)}) collective-permute-start(f32[4,4,1024]{2,1,0:T(4,128)S(1)} %get-tuple-element.53), channel_id=1, source_target_pairs={{0,8},{8,16},{16,24},{24,32},{32,40},{40,48},{48,56},{56,64},{64,7... | collective-permute-start | bytes 196616 | tf_op jit(solution)/shard_map/ppermute | solution.py:25
  193.8 5.6 %collective-permute-start.5 = (f32[4,4,1024]{2,1,0:T(4,128)S(1)}, f32[4,4,1024]{2,1,0:T(4,128)S(1)}, u32[]{:S(2)}, u32[]{:S(2)}) collective-permute-start(f32[4,4,1024]{2,1,0:T(4,128)S(1)} %get-tuple-element.54), channel_id=1, source_target_pairs={{8,0},{16,8},{24,16},{32,24},{40,32},{48,40},{56,48},{64,56},{72,6... | collective-permute-start | bytes 196616 | tf_op jit(solution)/shard_map/ppermute | solution.py:26
  200.4 5.9 %collective-permute-start.6 = (f32[4,264,4]{1,2,0:T(4,128)S(1)}, f32[4,264,4]{1,2,0:T(4,128)S(1)}, u32[]{:S(2)}, u32[]{:S(2)}) collective-permute-start(f32[4,264,4]{1,2,0:T(4,128)S(1)} %copy.32), channel_id=1, source_target_pairs={{0,1},{1,2},{2,3},{3,4},{4,5},{5,6},{6,7},{8,9},{9,10},{10,11},{11... | collective-permute-start | bytes 50696 | tf_op jit(solution)/shard_map/ppermute | solution.py:25
  204.8 4.8 %collective-permute-start.7 = (f32[4,264,4]{1,2,0:T(4,128)S(1)}, f32[4,264,4]{1,2,0:T(4,128)S(1)}, u32[]{:S(2)}, u32[]{:S(2)}) collective-permute-start(f32[4,264,4]{1,2,0:T(4,128)S(1)} %copy.34), channel_id=1, source_target_pairs={{1,0},{2,1},{3,2},{4,3},{5,4},{6,5},{7,6},{9,8},{10,9},{11,10},{12... | collective-permute-start | bytes 50696 | tf_op jit(solution)/shard_map/ppermute | solution.py:26
  327.3 4.4 collective-permute-start.8
  329.3 4.9 %collective-permute-start.9 = (f32[4,1,64]{2,1,0:T(1,128)S(1)}, f32[4,1,64]{2,1,0:T(1,128)S(1)}, u32[]{:S(2)}, u32[]{:S(2)}) collective-permute-start(f32[4,1,64]{2,1,0:T(1,128)S(1)} %get-tuple-element.60), channel_id=1, source_target_pairs={{8,0},{16,8},{24,16},{32,24},{40,32},{48,40},{56,48},{64,56},{72,6... | collective-permute-start | bytes 3080 | tf_op jit(solution)/shard_map/ppermute | solution.py:26
  334.3 3.4 collective-permute-start.10
  336.1 4.8 %collective-permute-start.11 = (f32[4,18,1]{2,1,0:T(8,128)S(1)}, f32[4,18,1]{2,1,0:T(8,128)S(1)}, u32[]{:S(2)}, u32[]{:S(2)}) collective-permute-start(f32[4,18,1]{2,1,0:T(8,128)S(1)} %get-tuple-element.58), channel_id=1, source_target_pairs={{1,0},{2,1},{3,2},{4,3},{5,4},{6,5},{7,6},{9,8},{10,9},{11,10},{12... | collective-permute-start | bytes 872 | tf_op jit(solution)/shard_map/ppermute | solution.py:26
  347.5 8.5 %copy-start.1 = (f32[4,256,1024]{2,1,0:T(8,128)}, f32[4,256,1024]{2,1,0:T(8,128)S(1)}, u32[]{:S(2)}) copy-start(f32[4,256,1024]{2,1,0:T(8,128)S(1)} %convolution_subtract_fusion) | copy-start | bytes 12582916
  347.5 5.3 %collective-permute-start.12 = (f32[4,1,1024]{2,1,0:T(1,128)S(1)}, f32[4,1,1024]{2,1,0:T(1,128)S(1)}, u32[]{:S(2)}, u32[]{:S(2)}) collective-permute-start(f32[4,1,1024]{2,1,0:T(1,128)S(1)} %get-tuple-element.52), channel_id=1, source_target_pairs={{0,8},{8,16},{16,24},{24,32},{32,40},{40,48},{48,56},{56,64},{64,7... | collective-permute-start | bytes 49160 | tf_op jit(solution)/shard_map/ppermute | solution.py:25
  350.9 5.1 %collective-permute-start.13 = (f32[4,1,1024]{2,1,0:T(1,128)S(1)}, f32[4,1,1024]{2,1,0:T(1,128)S(1)}, u32[]{:S(2)}, u32[]{:S(2)}) collective-permute-start(f32[4,1,1024]{2,1,0:T(1,128)S(1)} %get-tuple-element.51), channel_id=1, source_target_pairs={{8,0},{16,8},{24,16},{32,24},{40,32},{48,40},{56,48},{64,56},{72,6... | collective-permute-start | bytes 49160 | tf_op jit(solution)/shard_map/ppermute | solution.py:26
  356.5 5.6 %collective-permute-start.14 = (f32[4,258,1]{1,0,2:T(4,128)S(1)}, f32[4,258,1]{1,0,2:T(4,128)S(1)}, u32[]{:S(2)}, u32[]{:S(2)}) collective-permute-start(f32[4,258,1]{1,0,2:T(4,128)S(1)} %copy.38), channel_id=1, source_target_pairs={{1,0},{2,1},{3,2},{4,3},{5,4},{6,5},{7,6},{9,8},{10,9},{11,10},{12... | collective-permute-start | bytes 12392 | tf_op jit(solution)/shard_map/ppermute | solution.py:26
  358.1 4.8 %collective-permute-start.15 = (f32[4,258,1]{1,0,2:T(4,128)S(1)}, f32[4,258,1]{1,0,2:T(4,128)S(1)}, u32[]{:S(2)}, u32[]{:S(2)}) collective-permute-start(f32[4,258,1]{1,0,2:T(4,128)S(1)} %copy.40), channel_id=1, source_target_pairs={{0,1},{1,2},{2,3},{3,4},{4,5},{5,6},{6,7},{8,9},{9,10},{10,11},{11... | collective-permute-start | bytes 12392 | tf_op jit(solution)/shard_map/ppermute | solution.py:25
where the time goes:
time: 458 us; the launch traced here: 456 us
  blocking collectives  134 us (29%)
  other arithmetic  102 us (22%)
  local copies, waits for them, and re-layouts  83.4 us (18%)
  waiting for transfers between devices  71.2 us (16%)
  starting transfers between devices  55.5 us (12%)
  matrix products  8.74 us (2%)
    psum x1, blocking collectives, body(): height_all, slope_all = lax.psum((height_sq, slope_sum), ('row', 'col'))  78.1 us
    ppermute x8, waiting for transfers between devices, with_halo(): before = lax.ppermute(last, axis, up)  54.4 us
    ppermute x8, starting transfers between devices, with_halo(): before = lax.ppermute(last, axis, up)  41.4 us
    concatenate x4, other arithmetic, with_halo(): value = jnp.concatenate([before, value, after], axis=dim)  37.5 us
    all_gather x1, blocking collectives, long_cols(): portion = lax.all_gather(coarse, 'col', axis=2, tiled=True)  27.9 us
    all_gather x1, blocking collectives, long_rows(): portion = lax.all_gather(surface, 'row', axis=1, tiled=True)  27.6 us
    unnamed x18, local copies, waits for them, and re-layouts  24.7 us
    gather x12, local copies, waits for them, and re-layouts  21.5 us
  transfers between devices with their start and end apart: 16, of which 9 were waited for; matrix products, arithmetic and copies ran while one was open for 4% of the time, Pallas kernels for 0%

commit v1 on v0

--- a/solution.py
+++ b/solution.py
@@ -201,7 +201,7 @@
     slope_field = slopes(band_field)
     height_sq = jnp.sum(band_field * band_field, axis=(1, 2))
     slope_sum = jnp.sum(slope_field, axis=(1, 2))
-    height_all, slope_all = lax.psum((height_sq, slope_sum), ("row", "col"))
+    height_all, slope_all = lax.psum(lax.psum((height_sq, slope_sum), "row"), "col")
     total_cells = height * lax.axis_size("row") * length * lax.axis_size("col")
     surface_params = jnp.sqrt(jnp.stack([height_all, slope_all]) / total_cells + EPSILON)
     return (band_field, slope_field, surface_params)

time: 458 us -> 445 us (0.972)
  the two profiles are of different devices: /device:TPU:1 before, /device:TPU:64 now
where the time goes in v1:
time: 445 us; the launch traced here: 443 us
  blocking collectives  111 us (25%)
  other arithmetic  102 us (23%)
  local copies, waits for them, and re-layouts  83.1 us (19%)
  waiting for transfers between devices  79.9 us (18%)
  starting transfers between devices  56.6 us (13%)
  matrix products  8.74 us (2%)
    ppermute x8, waiting for transfers between devices, with_halo(): before = lax.ppermute(last, axis, up)  66.9 us
    concatenate x4, other arithmetic, with_halo(): value = jnp.concatenate([before, value, after], axis=dim)  37.5 us
    psum x1, blocking collectives, body(): lax.psum((height_sq, slope_sum), 'row')  37.2 us
    ppermute x8, starting transfers between devices, with_halo(): after = lax.ppermute(leading, axis, down)  34.6 us
    all_gather x1, blocking collectives, long_cols(): portion = lax.all_gather(coarse, 'col', axis=2, tiled=True)  32.9 us
    unnamed x18, local copies, waits for them, and re-layouts  24.7 us
    ppermute x8, starting transfers between devices, with_halo(): before = lax.ppermute(last, axis, up)  21.9 us
    gather x12, local copies, waits for them, and re-layouts  21.3 us
  transfers between devices with their start and end apart: 16, of which 9 were waited for; matrix products, arithmetic and copies ran while one was open for 4% of the time, Pallas kernels for 0%

profile of v1, /device:TPU:64, one launch (start us, length us, event | category | flops | bytes accessed | tf_op | source)
XLA Modules:
  0.0 442.8 jit_solution(17249186090269748911)
XLA Ops:
  9.9 7.4 %collective-permute-start.1 = (f32[4,130,1024]{2,0,1:T(4,128)}, f32[4,130,1024]{2,0,1:T(4,128)}, u32[]{:S(2)}, u32[]{:S(2)}) collective-permute-start(f32[4,130,1024]{2,0,1:T(4,128)} %copy.43), channel_id=1, source_target_pairs={{8,0},{16,8},{24,16},{32,24},{40,32},{48,40},{56,48},{64,56},{72,6... | collective-permute-start | bytes 6389768 | tf_op jit(solution)/shard_map/ppermute | solution.py:26
  17.3 5.2 %copy.28 = f32[4,256,1024]{1,0,2:T(4,128)} copy(f32[4,256,1024]{2,1,0:T(8,128)} %param.5) | data formatting | bytes 8388608 | tf_op args[1]
  22.7 14.0 %collective-permute-done = f32[4,130,1024]{2,0,1:T(4,128)} collective-permute-done((f32[4,130,1024]{2,0,1:T(4,128)S(1)}, f32[4,130,1024]{2,0,1:T(4,128)}, u32[]{:S(2)}, u32[]{:S(2)}) %collective-permute-start) | collective-permute-done | bytes 2129952 | tf_op jit(solution)/shard_map/ppermute | solution.py:25
  36.7 6.3 %copy.27 = f32[4,130,1024]{1,0,2:T(4,128)} copy(f32[4,130,1024]{2,0,1:T(4,128)} %collective-permute-done) | data formatting | bytes 4259840 | tf_op jit(solution)/shard_map/ppermute | solution.py:25
  42.9 6.2 %copy.29 = f32[4,130,1024]{1,0,2:T(4,128)} copy(f32[4,130,1024]{2,0,1:T(4,128)} %collective-permute-done.1) | data formatting | bytes 4259840 | tf_op jit(solution)/shard_map/ppermute | solution.py:26
  58.3 51.6 %collective-permute-done.2 = f32[4,516,130]{1,0,2:T(4,128)S(1)} collective-permute-done((f32[4,516,130]{1,0,2:T(4,128)S(1)}, f32[4,516,130]{1,0,2:T(4,128)S(1)}, u32[]{:S(2)}, u32[]{:S(2)}) %collective-permute-start.2) | collective-permute-done | bytes 1073312 | tf_op jit(solution)/shard_map/ppermute | solution.py:25
  110.0 29.5 %pad_maximum_fusion = f32[4,516,1284]{1,0,2:T(4,128)} fusion(f32[4,516,130]{1,0,2:T(4,128)S(1)} %collective-permute-done.3, f32[4,130,1024]{1,0,2:T(4,128)} %copy.29, f32[4,256,1024]{1,0,2:T(4,128)S(1)} %copy-done.2, f32[4,130,1024]{1,0,2:T(4,128)} %copy.27, f32[4,516,130]{1,0,2:T(4,128)S(1)} %collective-permute-done.2), kind=kLoop, calls=%fused_computation.2 | loop fusion | flops 10600704 | bytes 21201408 | tf_op jit(solution)/shard_map/concatenate | solution.py:27
  139.5 15.3 %copy.30 = f32[4,516,1284]{2,1,0:T(8,128)} copy(f32[4,516,1284]{1,0,2:T(4,128)} %pad_maximum_fusion) | data formatting | bytes 21201408
  154.7 21.3 %while.1 = (s32[]{:T(128)}, f32[4,516,1284]{2,1,0:T(8,128)}, s32[4,3]{1,0:T(4,128)S(1)}, f32[4,259,1027]{2,1,0:T(8,128)}, s32[]{:T(128)}) while((s32[]{:T(128)}, f32[4,516,1284]{2,1,0:T(8,128)}, s32[4,3]{1,0:T(4,128)S(1)}, f32[4,259,1027]{2,1,0:T(8,128)}, s32[]{:T(128)}) %tuple.51), condition=%wide.while_cond, body=%wide.while_body.sunk | while | flops 2 | bytes 2435185 | solution.py:68
  155.3 4.8 %dynamic-slice_dynamic-update-slice_fusion.2 = f32[4,259,1027]{2,1,0:T(8,128)} fusion(f32[4,259,1027]{2,1,0:T(8,128)} %get-tuple-element.120, s32[]{:T(128)} %get-tuple-element.117, f32[4,516,1284]{2,1,0:T(8,128)} %get-tuple-element.123, s32[]{:T(128)} %bitcast.84, s32[]{:T(128)} %bitcast.85, s32[]{:T(128)} %bitcast.86), kind=kLoop, calls=%fused_computation.clone.1 | loop fusion | bytes 2435072 | tf_op jit(solution)/shard_map/vmap()/gather
  160.7 4.7 %dynamic-slice_dynamic-update-slice_fusion.2 = f32[4,259,1027]{2,1,0:T(8,128)} fusion(f32[4,259,1027]{2,1,0:T(8,128)} %get-tuple-element.120, s32[]{:T(128)} %get-tuple-element.117, f32[4,516,1284]{2,1,0:T(8,128)} %get-tuple-element.123, s32[]{:T(128)} %bitcast.84, s32[]{:T(128)} %bitcast.85, s32[]{:T(128)} %bitcast.86), kind=kLoop, calls=%fused_computation.clone.1 | loop fusion | bytes 2435072 | tf_op jit(solution)/shard_map/vmap()/gather
  166.0 4.7 %dynamic-slice_dynamic-update-slice_fusion.2 = f32[4,259,1027]{2,1,0:T(8,128)} fusion(f32[4,259,1027]{2,1,0:T(8,128)} %get-tuple-element.120, s32[]{:T(128)} %get-tuple-element.117, f32[4,516,1284]{2,1,0:T(8,128)} %get-tuple-element.123, s32[]{:T(128)} %bitcast.84, s32[]{:T(128)} %bitcast.85, s32[]{:T(128)} %bitcast.86), kind=kLoop, calls=%fused_computation.clone.1 | loop fusion | bytes 2435072 | tf_op jit(solution)/shard_map/vmap()/gather
  171.3 4.7 %dynamic-slice_dynamic-update-slice_fusion.2 = f32[4,259,1027]{2,1,0:T(8,128)} fusion(f32[4,259,1027]{2,1,0:T(8,128)} %get-tuple-element.120, s32[]{:T(128)} %get-tuple-element.117, f32[4,516,1284]{2,1,0:T(8,128)} %get-tuple-element.123, s32[]{:T(128)} %bitcast.84, s32[]{:T(128)} %bitcast.85, s32[]{:T(128)} %bitcast.86), kind=kLoop, calls=%fused_computation.clone.1 | loop fusion | bytes 2435072 | tf_op jit(solution)/shard_map/vmap()/gather
  176.1 9.2 %multiply_add_fusion = f32[4,256,1027]{2,1,0:T(8,128)S(1)} fusion(f32[4,259,1027]{2,1,0:T(8,128)} %get-tuple-element.10, f32[4]{0:T(128)S(1)} %get-tuple-element.69, f32[4]{0:T(128)S(1)} %get-tuple-element.64, f32[4]{0:T(128)S(1)} %get-tuple-element.66, f32[4]{0:T(128)S(1)} %get-tuple-element.65), kind=kLoop, calls=%fused_computation.5 | loop fusion | flops 7361536 | bytes 21033024 | tf_op jit(solution)/shard_map/vmap()/add | solution.py:47
  190.7 7.3 %collective-permute-start.5 = (f32[4,4,1024]{2,1,0:T(4,128)S(1)}, f32[4,4,1024]{2,1,0:T(4,128)S(1)}, u32[]{:S(2)}, u32[]{:S(2)}) collective-permute-start(f32[4,4,1024]{2,1,0:T(4,128)S(1)} %get-tuple-element.56), channel_id=1, source_target_pairs={{8,0},{16,8},{24,16},{32,24},{40,32},{48,40},{56,48},{64,56},{72,6... | collective-permute-start | bytes 196616 | tf_op jit(solution)/shard_map/ppermute | solution.py:26
  200.9 4.4 collective-permute-start.6
  207.4 4.2 collective-permute-done.7
  211.8 7.4 %maximum_maximum_fusion = (f32[4,264,1028]{2,1,0:T(8,128)S(1)}, f32[4,264,1028]{2,1,0:T(8,128)}) fusion(f32[4,4,1024]{2,1,0:T(4,128)S(1)} %collective-permute-done.5, f32[4,256,1024]{2,1,0:T(8,128)} %copy-done, f32[4,4,1024]{2,1,0:T(4,128)S(1)} %collective-permute-done.4, f32[4,264,4]{2,1,0:T(8,128)S(1)} %copy.33, f32[4,264,4]{2,1,0:T(8,128)S(1)} %copy.35), kind=kLoop, calls=%fused_computation.3 | loop fusion | flops 6513408 | bytes 13043712 | tf_op jit(solution)/shard_map/concatenate | solution.py:27
  219.3 15.3 %fusion.1 = f32[4,264,1024]{2,1,0:T(8,128)S(1)} fusion(f32[4,264,1028]{2,1,0:T(8,128)} %get-tuple-element.47, f32[4,264,1028]{2,1,0:T(8,128)S(1)} %get-tuple-element.46, f32[1024]{0:T(1024)S(1)} %fusion.80, f32[4,4,1024]{2,1,0:T(4,128)S(1)} %collective-permute-done.5, f32[4,256,1024]{2,1,0:T(8,128)} %copy-done, f32[4,4,1024]{2,1,0:T(4,128)S(1)} %collective-permute-done.4), kind=kLoop, calls=%fused_computation.8 | loop fusion | flops 20545536 | bytes 43257856 | tf_op jit(solution)/shard_map/div | solution.py:95
  234.6 5.7 %fusion.17 = f32[4,256,1024]{2,1,0:T(8,128)} fusion(f32[4,264,1024]{2,1,0:T(8,128)S(1)} %fusion.1, f32[256]{0:T(256)S(1)} %multiply_add_fusion.3), kind=kLoop, calls=%fused_computation.41 | loop fusion | flops 17825792 | bytes 41944064 | tf_op jit(solution)/shard_map/div | solution.py:105
  240.2 19.0 %reshape.249 = f32[4,16,16,64,16]{4,3,2,1,0:T(8,128)} reshape(f32[4,256,1024]{2,1,0:T(8,128)} %fusion.17) | data formatting | bytes 8388608 | tf_op jit(solution)/shard_map/reshape | solution.py:110
  259.2 12.2 %reduce_sum.45 = f32[4,16,64]{2,1,0:T(8,128)S(1)} reduce(f32[4,16,16,64,16]{4,3,2,1,0:T(8,128)} %reshape.249, f32[]{:T(128)} %constant.64.clone.1), dimensions={2,4}, to_apply=%region_0.0 | reduce | flops 1044480 | bytes 4210692 | tf_op jit(solution)/shard_map/reduce_sum | solution.py:110
  271.5 32.9 %all_gather.6 = f32[4,16,512]{1,0,2:T(4,128)S(1)} all-gather(f32[4,16,64]{1,0,2:T(4,128)S(1)} %copy.36), channel_id=1, replica_groups=mesh['row'=16,'col'=8] {'col'}, dimensions={2}, use_global_device_ids=true | all-gather | bytes 147456 | tf_op jit(solution)/shard_map/all_gather | solution.py:121
  306.2 20.5 %all_gather.7 = f32[4,256,64]{2,1,0:T(8,128)S(1)} all-gather(f32[4,16,64]{2,1,0:T(8,128)S(1)} %convolution_divide_fusion), channel_id=1, replica_groups=mesh['row'=16,'col'=8] {'row'}, dimensions={1}, use_global_device_ids=true | all-gather | bytes 278528 | tf_op jit(solution)/shard_map/all_gather | solution.py:132
  329.5 6.9 %collective-permute-start.9 = (f32[4,1,64]{2,1,0:T(1,128)S(1)}, f32[4,1,64]{2,1,0:T(1,128)S(1)}, u32[]{:S(2)}, u32[]{:S(2)}) collective-permute-start(f32[4,1,64]{2,1,0:T(1,128)S(1)} %get-tuple-element.62), channel_id=1, source_target_pairs={{8,0},{16,8},{24,16},{32,24},{40,32},{48,40},{56,48},{64,56},{72,6... | collective-permute-start | bytes 3080 | tf_op jit(solution)/shard_map/ppermute | solution.py:26
  340.8 4.3 collective-permute-done.11
  345.6 6.0 %convolution_subtract_fusion = f32[4,256,1024]{2,1,0:T(8,128)S(1)} fusion(f32[4,256,1024]{2,1,0:T(8,128)} %fusion.17, f32[4,256,66]{1,2,0:T(8,128)S(1)} %convolution_bitcast_fusion, f32[1024]{0:T(1024)S(1)} %get-tuple-element.73, s32[1024]{0:T(1024)S(1)} %get-tuple-element.76, f32[1024]{0:T(1024)S(1)} %get-tuple-element.74, ...), kind=kOutput, calls=%fused_computation.65 | convolution fusion | flops 831858688 | bytes 8675592 | tf_op jit(solution)/shard_map/spb,qb->spq/dot_general | solution.py:170
  353.6 7.3 %collective-permute-start.13 = (f32[4,1,1024]{2,1,0:T(1,128)S(1)}, f32[4,1,1024]{2,1,0:T(1,128)S(1)}, u32[]{:S(2)}, u32[]{:S(2)}) collective-permute-start(f32[4,1,1024]{2,1,0:T(1,128)S(1)} %get-tuple-element.53), channel_id=1, source_target_pairs={{8,0},{16,8},{24,16},{32,24},{40,32},{48,40},{56,48},{64,56},{72,6... | collective-permute-start | bytes 49160 | tf_op jit(solution)/shard_map/ppermute | solution.py:26
  364.3 4.6 %collective-permute-start.15 = (f32[4,258,1]{1,0,2:T(4,128)S(1)}, f32[4,258,1]{1,0,2:T(4,128)S(1)}, u32[]{:S(2)}, u32[]{:S(2)}) collective-permute-start(f32[4,258,1]{1,0,2:T(4,128)S(1)} %copy.40), channel_id=1, source_target_pairs={{0,1},{1,2},{2,3},{3,4},{4,5},{5,6},{6,7},{8,9},{9,10},{10,11},{11... | collective-permute-start | bytes 12392 | tf_op jit(solution)/shard_map/ppermute | solution.py:25
  370.5 13.9 %fusion.112 = (f32[4]{0:T(128)S(1)}, f32[4,256,1024]{2,1,0:T(8,128)}, f32[4]{0:T(128)S(1)}) fusion(f32[256]{0:T(256)S(1)} %and_convert_fusion, f32[4,256,1024]{2,1,0:T(8,128)} %copy-done.1, f32[4,1,1024]{2,1,0:T(1,128)S(1)} %collective-permute-done.12, f32[4,1,1024]{2,1,0:T(1,128)S(1)} %collective-permute-done.13, f32[1024]{0:T(1024)S(1)} %fusion.92, ...), kind=kLoop, calls=%fused_computation.219 | loop fusion | flops 18874360 | bytes 8434784 | tf_op jit(solution)/shard_map/reduce_sum | solution.py:203
  384.4 37.2 %all-reduce = (f32[4]{0:T(128)S(1)}, f32[4]{0:T(128)S(1)}) all-reduce(f32[4]{0:T(128)S(1)} %get-tuple-element.39, f32[4]{0:T(128)S(1)} %get-tuple-element.52), channel_id=1, replica_groups=mesh['row'=16,'col'=8] {'row'}, use_global_device_ids=true, to_apply=%region_7.8 | all-reduce | flops 8 | bytes 64 | tf_op jit(solution)/shard_map/psum | solution.py:204
  421.7 20.6 %all-reduce.1 = (f32[1,4]{1,0:T(1,128)S(1)}, f32[1,4]{1,0:T(1,128)S(1)}) all-reduce(f32[1,4]{1,0:T(1,128)S(1)} %bitcast.87, f32[1,4]{1,0:T(1,128)S(1)} %bitcast.88), channel_id=1, replica_groups=mesh['row'=16,'col'=8] {'col'}, use_global_device_ids=true, to_apply=%region_8.9 | all-reduce | flops 8 | bytes 64 | tf_op jit(solution)/shard_map/psum | solution.py:204
  (91 shorter events, 48.6 us)
Async XLA Ops:
  5.3 31.4 %collective-permute-start = (f32[4,130,1024]{2,0,1:T(4,128)S(1)}, f32[4,130,1024]{2,0,1:T(4,128)}, u32[]{:S(2)}, u32[]{:S(2)}) collective-permute-start(f32[4,130,1024]{2,0,1:T(4,128)S(1)} %copy.42), channel_id=1, source_target_pairs={{0,8},{8,16},{16,24},{24,32},{32,40},{40,48},{48,56},{56,64},{64,7... | collective-permute-start | bytes 6389768 | tf_op jit(solution)/shard_map/ppermute | solution.py:25
  9.9 12.6 %copy-start.5 = (s32[2,4,1,1]{1,3,2,0:T(1,128)S(1)}, s32[2,4,1,1]{1,3,2,0:T(1,128)}, u32[]{:S(2)}) copy-start(s32[2,4,1,1]{1,3,2,0:T(1,128)} %param.6) | copy-start | bytes 100
  9.9 33.0 %collective-permute-start.1 = (f32[4,130,1024]{2,0,1:T(4,128)}, f32[4,130,1024]{2,0,1:T(4,128)}, u32[]{:S(2)}, u32[]{:S(2)}) collective-permute-start(f32[4,130,1024]{2,0,1:T(4,128)} %copy.43), channel_id=1, source_target_pairs={{8,0},{16,8},{24,16},{32,24},{40,32},{48,40},{56,48},{64,56},{72,6... | collective-permute-start | bytes 6389768 | tf_op jit(solution)/shard_map/ppermute | solution.py:26
  49.1 9.1 %copy-start.4 = (s32[2,4,1,1]{1,3,2,0:T(1,128)S(1)}, s32[2,4,1,1]{1,3,2,0:T(1,128)}, u32[]{:S(2)}) copy-start(s32[2,4,1,1]{1,3,2,0:T(1,128)} %param.7) | copy-start | bytes 100
  49.1 60.9 %copy-start.2 = (f32[4,256,1024]{1,0,2:T(4,128)S(1)}, f32[4,256,1024]{1,0,2:T(4,128)}, u32[]{:S(2)}) copy-start(f32[4,256,1024]{1,0,2:T(4,128)} %copy.28) | copy-start | bytes 12582916
  52.6 57.4 %collective-permute-start.2 = (f32[4,516,130]{1,0,2:T(4,128)S(1)}, f32[4,516,130]{1,0,2:T(4,128)S(1)}, u32[]{:S(2)}, u32[]{:S(2)}) collective-permute-start(f32[4,516,130]{1,0,2:T(4,128)S(1)} %get-tuple-element.44), channel_id=1, source_target_pairs={{0,1},{1,2},{2,3},{3,4},{4,5},{5,6},{6,7},{8,9},{9,10},{10,11},{11... | collective-permute-start | bytes 3219848 | tf_op jit(solution)/shard_map/ppermute | solution.py:25
  56.2 53.8 %collective-permute-start.3 = (f32[4,516,130]{1,0,2:T(4,128)S(1)}, f32[4,516,130]{1,0,2:T(4,128)S(1)}, u32[]{:S(2)}, u32[]{:S(2)}) collective-permute-start(f32[4,516,130]{1,0,2:T(4,128)S(1)} %get-tuple-element.45), channel_id=1, source_target_pairs={{1,0},{2,1},{3,2},{4,3},{5,4},{6,5},{7,6},{9,8},{10,9},{11,10},{12... | collective-permute-start | bytes 3219848 | tf_op jit(solution)/shard_map/ppermute | solution.py:26
  176.1 9.2 %copy-start.3 = (f32[4,256,1024]{2,1,0:T(8,128)S(1)}, f32[4,256,1024]{2,1,0:T(8,128)}, u32[]{:S(2)}) copy-start(f32[4,256,1024]{2,1,0:T(8,128)} %param.4) | copy-start | bytes 12582916
  188.7 11.7 %copy-start = (f32[4,256,1024]{2,1,0:T(8,128)}, f32[4,256,1024]{2,1,0:T(8,128)S(1)}, u32[]{:S(2)}) copy-start(f32[4,256,1024]{2,1,0:T(8,128)S(1)} %fusion.25) | copy-start | bytes 12582916
  188.8 9.2 %collective-permute-start.4 = (f32[4,4,1024]{2,1,0:T(4,128)S(1)}, f32[4,4,1024]{2,1,0:T(4,128)S(1)}, u32[]{:S(2)}, u32[]{:S(2)}) collective-permute-start(f32[4,4,1024]{2,1,0:T(4,128)S(1)} %get-tuple-element.55), channel_id=1, source_target_pairs={{0,8},{8,16},{16,24},{24,32},{32,40},{40,48},{48,56},{56,64},{64,7... | collective-permute-start | bytes 196616 | tf_op jit(solution)/shard_map/ppermute | solution.py:25
  190.7 9.1 %collective-permute-start.5 = (f32[4,4,1024]{2,1,0:T(4,128)S(1)}, f32[4,4,1024]{2,1,0:T(4,128)S(1)}, u32[]{:S(2)}, u32[]{:S(2)}) collective-permute-start(f32[4,4,1024]{2,1,0:T(4,128)S(1)} %get-tuple-element.56), channel_id=1, source_target_pairs={{8,0},{16,8},{24,16},{32,24},{40,32},{48,40},{56,48},{64,56},{72,6... | collective-permute-start | bytes 196616 | tf_op jit(solution)/shard_map/ppermute | solution.py:26
  200.9 6.2 %collective-permute-start.6 = (f32[4,264,4]{1,2,0:T(4,128)S(1)}, f32[4,264,4]{1,2,0:T(4,128)S(1)}, u32[]{:S(2)}, u32[]{:S(2)}) collective-permute-start(f32[4,264,4]{1,2,0:T(4,128)S(1)} %copy.32), channel_id=1, source_target_pairs={{0,1},{1,2},{2,3},{3,4},{4,5},{5,6},{6,7},{8,9},{9,10},{10,11},{11... | collective-permute-start | bytes 50696 | tf_op jit(solution)/shard_map/ppermute | solution.py:25
  205.6 6.0 %collective-permute-start.7 = (f32[4,264,4]{1,2,0:T(4,128)S(1)}, f32[4,264,4]{1,2,0:T(4,128)S(1)}, u32[]{:S(2)}, u32[]{:S(2)}) collective-permute-start(f32[4,264,4]{1,2,0:T(4,128)S(1)} %copy.34), channel_id=1, source_target_pairs={{1,0},{2,1},{3,2},{4,3},{5,4},{6,5},{7,6},{9,8},{10,9},{11,10},{12... | collective-permute-start | bytes 50696 | tf_op jit(solution)/shard_map/ppermute | solution.py:26
  327.2 9.2 %collective-permute-start.8 = (f32[4,1,64]{2,1,0:T(1,128)S(1)}, f32[4,1,64]{2,1,0:T(1,128)S(1)}, u32[]{:S(2)}, u32[]{:S(2)}) collective-permute-start(f32[4,1,64]{2,1,0:T(1,128)S(1)} %get-tuple-element.61), channel_id=1, source_target_pairs={{0,8},{8,16},{16,24},{24,32},{32,40},{40,48},{48,56},{56,64},{64,7... | collective-permute-start | bytes 3080 | tf_op jit(solution)/shard_map/ppermute | solution.py:25
  329.5 8.2 %collective-permute-start.9 = (f32[4,1,64]{2,1,0:T(1,128)S(1)}, f32[4,1,64]{2,1,0:T(1,128)S(1)}, u32[]{:S(2)}, u32[]{:S(2)}) collective-permute-start(f32[4,1,64]{2,1,0:T(1,128)S(1)} %get-tuple-element.62), channel_id=1, source_target_pairs={{8,0},{16,8},{24,16},{32,24},{40,32},{48,40},{56,48},{64,56},{72,6... | collective-permute-start | bytes 3080 | tf_op jit(solution)/shard_map/ppermute | solution.py:26
  337.8 3.0 collective-permute-start.10
  339.1 6.0 %collective-permute-start.11 = (f32[4,18,1]{2,1,0:T(8,128)S(1)}, f32[4,18,1]{2,1,0:T(8,128)S(1)}, u32[]{:S(2)}, u32[]{:S(2)}) collective-permute-start(f32[4,18,1]{2,1,0:T(8,128)S(1)} %get-tuple-element.60), channel_id=1, source_target_pairs={{1,0},{2,1},{3,2},{4,3},{5,4},{6,5},{7,6},{9,8},{10,9},{11,10},{12... | collective-permute-start | bytes 872 | tf_op jit(solution)/shard_map/ppermute | solution.py:26
  351.6 10.7 %copy-start.1 = (f32[4,256,1024]{2,1,0:T(8,128)}, f32[4,256,1024]{2,1,0:T(8,128)S(1)}, u32[]{:S(2)}) copy-start(f32[4,256,1024]{2,1,0:T(8,128)S(1)} %convolution_subtract_fusion) | copy-start | bytes 12582916
  351.6 9.2 %collective-permute-start.12 = (f32[4,1,1024]{2,1,0:T(1,128)S(1)}, f32[4,1,1024]{2,1,0:T(1,128)S(1)}, u32[]{:S(2)}, u32[]{:S(2)}) collective-permute-start(f32[4,1,1024]{2,1,0:T(1,128)S(1)} %get-tuple-element.54), channel_id=1, source_target_pairs={{0,8},{8,16},{16,24},{24,32},{32,40},{40,48},{48,56},{56,64},{64,7... | collective-permute-start | bytes 49160 | tf_op jit(solution)/shard_map/ppermute | solution.py:25
  353.6 8.7 %collective-permute-start.13 = (f32[4,1,1024]{2,1,0:T(1,128)S(1)}, f32[4,1,1024]{2,1,0:T(1,128)S(1)}, u32[]{:S(2)}, u32[]{:S(2)}) collective-permute-start(f32[4,1,1024]{2,1,0:T(1,128)S(1)} %get-tuple-element.53), channel_id=1, source_target_pairs={{8,0},{16,8},{24,16},{32,24},{40,32},{48,40},{56,48},{64,56},{72,6... | collective-permute-start | bytes 49160 | tf_op jit(solution)/shard_map/ppermute | solution.py:26
  362.8 6.2 %collective-permute-start.14 = (f32[4,258,1]{1,0,2:T(4,128)S(1)}, f32[4,258,1]{1,0,2:T(4,128)S(1)}, u32[]{:S(2)}, u32[]{:S(2)}) collective-permute-start(f32[4,258,1]{1,0,2:T(4,128)S(1)} %copy.38), channel_id=1, source_target_pairs={{1,0},{2,1},{3,2},{4,3},{5,4},{6,5},{7,6},{9,8},{10,9},{11,10},{12... | collective-permute-start | bytes 12392 | tf_op jit(solution)/shard_map/ppermute | solution.py:26
  364.3 6.0 %collective-permute-start.15 = (f32[4,258,1]{1,0,2:T(4,128)S(1)}, f32[4,258,1]{1,0,2:T(4,128)S(1)}, u32[]{:S(2)}, u32[]{:S(2)}) collective-permute-start(f32[4,258,1]{1,0,2:T(4,128)S(1)} %copy.40), channel_id=1, source_target_pairs={{0,1},{1,2},{2,3},{3,4},{4,5},{5,6},{6,7},{8,9},{9,10},{10,11},{11... | collective-permute-start | bytes 12392 | tf_op jit(solution)/shard_map/ppermute | solution.py:25
